TPU v7x, 32 devices: a whole 2x2x4 slice. The times are simulated.
32 devices in a mesh: row: 8 (over z, x), col: 4 (over y, core).
Axes of the slice: x: 2, y: 2, z: 4, core: 2. Of those that a mesh axis runs over, the one named last changes fastest.
Arguments:
- alignment: bfloat16 [256, 192, 256], P('row', 'col'), may hold values from -8 to 8
- alignment_mask: int32 [256, 192], P('row', 'col'), may hold values from 0 to 1, as said below
- residue_mask: int32 [192], replicated, may hold values from 0 to 1, as said below
- pair_features: bfloat16 [192, 192, 128], P('row', 'col'), may hold values from -6 to 6
- outer_product_left: bfloat16 [256, 32], replicated, may hold values from -0.375 to 0.375
- outer_product_right: bfloat16 [256, 32], replicated, may hold values from -0.375 to 0.375
- outer_proj: bfloat16 [1024, 128], replicated, may hold values from -0.1875 to 0.1875
- triangle_proj: bfloat16 [128, 512], replicated, may hold values from -0.5 to 0.5
- triangle_gate: bfloat16 [128, 128], replicated, may hold values from -0.5 to 0.5
- triangle_out: bfloat16 [128, 128], replicated, may hold values from -0.5 to 0.5
- transition_in: bfloat16 [128, 512], replicated, may hold values from -0.5 to 0.5
- transition_out: bfloat16 [512, 128], replicated, may hold values from -0.25 to 0.25
Outputs:
- pair_out: bfloat16 [192, 192, 128], P('row', 'col')
Inputs may be any that keep to these rules, and one draw needn't show every extreme that they name: `residue_mask`: masked residues scattered anywhere; at least one residue is masked and at least one takes part. `alignment_mask`: 0 wherever residue_mask is 0.
All inputs are finite; a program needn't handle non-finite values.
Results may differ from a plain program's by a relative error of at most 0.014.
Values may be sent and summed in bfloat16 or wider, within the bound.
No kernel may reach another device: no remote copies, remote signals or barrier semaphores. Data moves between devices by JAX's collectives and lax.ppermute only.
A program may use at most 64 MiB of HBM per device.

v0:
```python
import jax
import jax.numpy as jnp
from jax import lax
from jax.sharding import PartitionSpec as P

epsilon = 1e-05


def normalize(values):
    mean_value = jnp.mean(values, axis=-1, keepdims=True)
    centered = values - mean_value
    variance = jnp.mean(centered * centered, axis=-1, keepdims=True)
    return centered * lax.rsqrt(variance + epsilon)


def shards(
    alignment,
    alignment_mask,
    residue_mask,
    pair_features,
    outer_product_left,
    outer_product_right,
    outer_proj,
    triangle_proj,
    triangle_gate,
    triangle_out,
    transition_in,
    transition_out,
):
    block_rows, block_cols, channels = pair_features.shape
    inner = triangle_out.shape[0]
    narrow = outer_product_left.shape[1]
    mask_float = alignment_mask.astype(jnp.float32)
    normed = normalize(alignment.astype(jnp.float32)).astype(jnp.bfloat16)
    left_side = (
        jnp.dot(normed, outer_product_left, preferred_element_type=jnp.float32)
        * mask_float[..., None]
    ).astype(jnp.bfloat16)
    right_side = (
        jnp.dot(normed, outer_product_right, preferred_element_type=jnp.float32)
        * mask_float[..., None]
    ).astype(jnp.bfloat16)
    mask_wire = alignment_mask.astype(jnp.bfloat16)
    right_all, right_mask = (
        lax.all_gather(right_side, "row", axis=0, tiled=True),
        lax.all_gather(mask_wire, "row", axis=0, tiled=True),
    )
    left_rows, left_row_mask = (
        lax.all_gather(left_side, "col", axis=1, tiled=True),
        lax.all_gather(mask_wire, "col", axis=1, tiled=True),
    )
    left_all, left_mask = (
        lax.all_to_all(left_rows, "row", split_axis=1, concat_axis=0, tiled=True),
        lax.all_to_all(left_row_mask, "row", split_axis=1, concat_axis=0, tiled=True),
    )
    sequences = left_all.shape[0]
    contract = (((0,), (0,)), ((), ()))
    outer = lax.dot_general(
        left_all.reshape(sequences, block_rows * narrow),
        right_all.reshape(sequences, block_cols * narrow),
        contract,
        preferred_element_type=jnp.float32,
    )
    outer = (
        outer.reshape(block_rows, narrow, block_cols, narrow)
        .transpose(0, 2, 1, 3)
        .astype(jnp.bfloat16)
    )
    outer = outer.reshape(block_rows, block_cols, narrow * narrow)
    projected = jnp.dot(outer, outer_proj, preferred_element_type=jnp.float32)
    counts = lax.dot_general(left_mask, right_mask, contract, preferred_element_type=jnp.float32)
    first = (
        pair_features.astype(jnp.float32) + projected / jnp.maximum(counts, 1.0)[..., None]
    ).astype(jnp.bfloat16)
    normed_pair = normalize(first.astype(jnp.float32)).astype(jnp.bfloat16)
    projections = jnp.dot(normed_pair, triangle_proj, preferred_element_type=jnp.float32)
    row_mask = lax.dynamic_slice_in_dim(
        residue_mask, lax.axis_index("row") * block_rows, block_rows
    ).astype(jnp.float32)
    col_mask = lax.dynamic_slice_in_dim(
        residue_mask, lax.axis_index("col") * block_cols, block_cols
    ).astype(jnp.float32)
    pair_mask = (row_mask[:, None] * col_mask[None, :])[..., None]
    left_tri = (
        jax.nn.sigmoid(projections[..., :inner]) * projections[..., inner : 2 * inner] * pair_mask
    ).astype(jnp.bfloat16)
    right_tri = (
        jax.nn.sigmoid(projections[..., 2 * inner : 3 * inner])
        * projections[..., 3 * inner :]
        * pair_mask
    ).astype(jnp.bfloat16)
    right_cols = lax.all_gather(right_tri, "row", axis=0, tiled=True)
    right_rows = lax.all_to_all(right_cols, "col", split_axis=0, concat_axis=1, tiled=True)
    summed = jnp.einsum(
        "ikc,jkc->ijc",
        lax.all_gather(left_tri, "col", axis=1, tiled=True),
        right_rows,
        preferred_element_type=jnp.float32,
    )
    normed_sum = normalize(summed).astype(jnp.bfloat16)
    update = jax.nn.sigmoid(
        jnp.dot(normed_pair, triangle_gate, preferred_element_type=jnp.float32)
    ) * jnp.dot(normed_sum, triangle_out, preferred_element_type=jnp.float32)
    second = (first.astype(jnp.float32) + update).astype(jnp.bfloat16)
    normed_second = normalize(second.astype(jnp.float32)).astype(jnp.bfloat16)
    hidden_units = jnp.maximum(
        jnp.dot(normed_second, transition_in, preferred_element_type=jnp.float32), 0.0
    ).astype(jnp.bfloat16)
    return (
        second.astype(jnp.float32)
        + jnp.dot(hidden_units, transition_out, preferred_element_type=jnp.float32)
    ).astype(jnp.bfloat16)


def solution(mesh):
    placed = (
        P("row", "col", None),
        P("row", "col"),
        P(),
        P("row", "col", None),
        P(),
        P(),
        P(),
        P(),
        P(),
        P(),
        P(),
        P(),
    )
    return jax.shard_map(
        shards, mesh=mesh, in_specs=placed, out_specs=P("row", "col", None), check_vma=False
    )
```

profile of v0, /device:TPU:0, one launch (start us, length us, event | category | flops | bytes accessed | tf_op | source)
XLA Modules:
  0.0 276.2 jit_solution(16021958013082864905)
XLA Ops:
  6.5 0.8 fusion.48
  7.4 6.2 %all-gather = bf16[4,48,32]{1,2,0:T(8,128)(2,1)S(1)} all-gather(bf16[1,48,32]{1,2,0:T(8,128)(2,1)S(1)} %bitcast.93), channel_id=1, replica_groups=mesh['row'=8,'col'=4] {'col'}, dimensions={0}, use_global_device_ids=true | all-gather | bytes 15360 | tf_op jit(solution)/shard_map/all_gather | solution.py:50
  13.8 0.7 reshape.110
  14.5 6.2 %all-to-all-start.1 = ((bf16[8,2,384]{2,1,0:T(2,128)(2,1)}), bf16[8,2,384]{2,1,0:T(2,128)(2,1)S(1)}, u32[]{:S(2)}, u32[]{:S(2)}) async-start(bf16[8,2,384]{2,1,0:T(2,128)(2,1)} %reshape.110), calls=%async_computation.1 | async-start | bytes 24576 | tf_op jit(solution)/shard_map/all_to_all | solution.py:54
  20.8 1.4 convert_reduce_fusion
  22.7 0.7 fusion.16
  24.1 13.4 %all_gather.18 = bf16[32,192,32]{2,0,1:T(8,128)(2,1)} all-gather(bf16[32,48,32]{2,0,1:T(8,128)(2,1)S(1)} %copy.51), channel_id=1, replica_groups=mesh['row'=8,'col'=4] {'col'}, dimensions={1}, use_global_device_ids=true | all-gather | bytes 491520 | tf_op jit(solution)/shard_map/all_gather | solution.py:49
  37.4 0.7 fusion.17
  38.1 45.3 %all_gather.19 = bf16[256,48,32]{1,2,0:T(8,128)(2,1)S(1)} all-gather(bf16[32,48,32]{1,2,0:T(8,128)(2,1)S(1)} %fusion.17), channel_id=1, replica_groups=mesh['row'=8,'col'=4] {'row'}, dimensions={0}, use_global_device_ids=true | all-gather | bytes 884736 | tf_op jit(solution)/shard_map/all_gather | solution.py:45
  83.6 3.8 %reshape.108 = bf16[8,2,12288]{2,1,0:T(2,128)(2,1)} reshape(bf16[192,32,32]{2,1,0:T(8,128)(2,1)} %bitcast.89) | data formatting | bytes 786432
  87.4 2.4 copy.56
  89.8 3.6 %all-to-all-start = ((bf16[8,2,12288]{2,1,0:T(2,128)(2,1)}), bf16[8,2,12288]{2,1,0:T(2,128)(2,1)S(1)}, u32[]{:S(2)}, u32[]{:S(2)}) async-start(bf16[8,2,12288]{2,1,0:T(2,128)(2,1)} %reshape.108), calls=%async_computation | async-start | bytes 786432 | tf_op jit(solution)/shard_map/all_to_all | solution.py:53
  93.4 35.2 %all_gather.21 = bf16[256,48]{1,0:T(8,128)(2,1)S(1)} all-gather(bf16[32,48]{1,0:T(8,128)(2,1)S(1)} %get-tuple-element.7), channel_id=1, replica_groups=mesh['row'=8,'col'=4] {'row'}, dimensions={0}, use_global_device_ids=true | all-gather | bytes 27648 | tf_op jit(solution)/shard_map/all_gather | solution.py:46
  129.0 0.8 reshape.109
  130.4 1.0 reshape.93
  131.6 3.7 %convert_bitcast_fusion = bf16[24,48,32,32]{1,2,3,0:T(8,128)(2,1)} fusion(bf16[24,32,256,1]{2,1,3,0:T(8,128)(2,1)S(1)} %bitcast.90, bf16[48,32,256]{2,0,1:T(8,128)(2,1)S(1)} %copy-done.4), kind=kOutput, calls=%fused_computation | convolution fusion | flops 605159424 | bytes 3538944 | tf_op jit(solution)/shard_map/dot_general | solution.py:58
  135.3 17.8 %copy.57 = bf16[24,48,32,32]{3,2,1,0:T(8,128)(2,1)} copy(bf16[24,48,32,32]{1,2,3,0:T(8,128)(2,1)} %convert_bitcast_fusion) | data formatting | bytes 4718592 | tf_op jit(solution)/shard_map/convert_element_type | solution.py:67
  153.1 12.7 %reshape.95 = bf16[24,48,1024]{2,1,0:T(8,128)(2,1)S(1)} reshape(bf16[24,48,32,32]{3,2,1,0:T(8,128)(2,1)} %copy.57) | data formatting | bytes 4718592 | tf_op jit(solution)/shard_map/reshape | solution.py:69
  165.9 1.8 fusion.49
  168.7 1.2 fusion.22
  170.0 0.7 all-gather.6.cloned.1.call-update
  170.7 48.0 %all-gather.4.cloned.1.call-done = bf16[192,48,128]{2,1,0:T(8,128)(2,1)} async-done(((bf16[24,48,128]{2,1,0:T(8,128)(2,1)}), bf16[192,48,128]{2,1,0:T(8,128)(2,1)}) %all-gather.4.cloned.1.call-update) | async-done | bytes 2359312 | tf_op jit(solution)/shard_map/all_gather | solution.py:92
  218.7 3.9 %all-to-all-start.2 = ((bf16[192,48,128]{2,1,0:T(8,128)(2,1)}), bf16[192,48,128]{2,1,0:T(8,128)(2,1)S(1)}, u32[]{:S(2)}, u32[]{:S(2)}) async-start(bf16[192,48,128]{2,1,0:T(8,128)(2,1)} %all-gather.4.cloned.1.call-done), calls=%async_computation.2 | async-start | bytes 4718592 | tf_op jit(solution)/shard_map/all_to_all | solution.py:93
  222.6 1.3 fusion.9
  223.9 18.8 %all-gather.6.cloned.1.call-done = bf16[24,192,128]{2,1,0:T(8,128)(2,1)} async-done(((bf16[24,48,128]{2,1,0:T(8,128)(2,1)}), bf16[24,192,128]{2,1,0:T(8,128)(2,1)}) %all-gather.6.cloned.1.call-update) | async-done | bytes 1179664 | tf_op jit(solution)/shard_map/all_gather | solution.py:96
  242.7 2.8 %copy.63 = bf16[24,192,128]{1,0,2:T(8,128)(2,1)} copy(bf16[24,192,128]{2,1,0:T(8,128)(2,1)} %all-gather.6.cloned.1.call-done) | data formatting | bytes 2359296 | tf_op jit(solution)/shard_map/all_gather | solution.py:96
  245.5 11.6 %all-to-all-done.2 = bf16[192,48,128]{2,1,0:T(8,128)(2,1)S(1)} async-done(((bf16[192,48,128]{2,1,0:T(8,128)(2,1)}), bf16[192,48,128]{2,1,0:T(8,128)(2,1)S(1)}, u32[]{:S(2)}, u32[]{:S(2)}) %all-to-all-start.2) | async-done | bytes 2359328 | tf_op jit(solution)/shard_map/all_to_all | solution.py:93
  257.1 2.1 copy.61
  259.2 3.8 %copy.62 = bf16[48,192,128]{1,0,2:T(8,128)(2,1)S(1)} copy(bf16[48,192,128]{2,1,0:T(8,128)(2,1)} %bitcast.86) | data formatting | bytes 4718592 | tf_op jit(solution)/shard_map/all_to_all | solution.py:93
  263.0 2.4 bitcast_reduce_fusion
  265.9 0.8 copy-done.2
  267.8 1.5 fusion.15
  (61 shorter events, 5.4 us)
Async XLA Ops:
  6.5 159.3 %copy-start = (bf16[1024,128]{1,0:T(8,128)(2,1)S(1)}, bf16[1024,128]{1,0:T(8,128)(2,1)}, u32[]{:S(2)}) copy-start(bf16[1024,128]{1,0:T(8,128)(2,1)} %param.18) | copy-start | bytes 786436
  6.5 15.7 %copy-start.3 = (bf16[32,48,256]{2,1,0:T(8,128)(2,1)S(1)}, bf16[32,48,256]{2,1,0:T(8,128)(2,1)}, u32[]{:S(2)}) copy-start(bf16[32,48,256]{2,1,0:T(8,128)(2,1)} %param.12) | copy-start | bytes 2359300
  6.5 16.2 %copy-start.11 = (bf16[256,32]{0,1:T(8,128)(2,1)S(1)}, bf16[256,32]{0,1:T(8,128)(2,1)}, u32[]{:S(2)}) copy-start(bf16[256,32]{0,1:T(8,128)(2,1)} %param.16) | copy-start | bytes 49156
  14.5 75.3 %all-to-all-start.1 = ((bf16[8,2,384]{2,1,0:T(2,128)(2,1)}), bf16[8,2,384]{2,1,0:T(2,128)(2,1)S(1)}, u32[]{:S(2)}, u32[]{:S(2)}) async-start(bf16[8,2,384]{2,1,0:T(2,128)(2,1)} %reshape.110), calls=%async_computation.1 | async-start | bytes 24576 | tf_op jit(solution)/shard_map/all_to_all | solution.py:54
  23.4 14.0 %copy-start.12 = (bf16[256,32]{0,1:T(8,128)(2,1)S(1)}, bf16[256,32]{0,1:T(8,128)(2,1)}, u32[]{:S(2)}) copy-start(bf16[256,32]{0,1:T(8,128)(2,1)} %param.17) | copy-start | bytes 49156
  38.1 45.4 %copy-start.13 = (s32[192]{0:T(256)S(1)}, s32[192]{0:T(256)}, u32[]{:S(2)}) copy-start(s32[192]{0:T(256)} %param.14) | copy-start | bytes 2308
  89.8 39.2 %all-to-all-start = ((bf16[8,2,12288]{2,1,0:T(2,128)(2,1)}), bf16[8,2,12288]{2,1,0:T(2,128)(2,1)S(1)}, u32[]{:S(2)}, u32[]{:S(2)}) async-start(bf16[8,2,12288]{2,1,0:T(2,128)(2,1)} %reshape.108), calls=%async_computation | async-start | bytes 786432 | tf_op jit(solution)/shard_map/all_to_all | solution.py:53
  93.4 125.3 %all-gather.4.cloned.1.call-start = ((), (), s32[]{:S(2)}) async-start(), calls=%async_computation.3 | async-start | bytes 2654208 | tf_op jit(solution)/shard_map/all_gather | solution.py:92
  130.4 1.2 copy-start.4
  165.9 2.3 copy-start.6
  167.7 54.8 %copy-start.1 = (f32[24,48,128]{2,1,0:T(8,128)}, f32[24,48,128]{2,1,0:T(8,128)S(1)}, u32[]{:S(2)}) copy-start(f32[24,48,128]{2,1,0:T(8,128)S(1)} %get-tuple-element.10) | copy-start | bytes 1769476
  169.9 72.8 %all-gather.6.cloned.1.call-start = ((), (), s32[]{:S(2)}) async-start(), calls=%async_computation.4 | async-start | bytes 1474560 | tf_op jit(solution)/shard_map/all_gather | solution.py:96
  170.7 51.9 %copy-start.10 = (bf16[128,128]{1,0:T(8,128)(2,1)S(1)}, bf16[128,128]{1,0:T(8,128)(2,1)}, u32[]{:S(2)}) copy-start(bf16[128,128]{1,0:T(8,128)(2,1)} %param.20) | copy-start | bytes 98308
  218.7 38.4 %all-to-all-start.2 = ((bf16[192,48,128]{2,1,0:T(8,128)(2,1)}), bf16[192,48,128]{2,1,0:T(8,128)(2,1)S(1)}, u32[]{:S(2)}, u32[]{:S(2)}) async-start(bf16[192,48,128]{2,1,0:T(8,128)(2,1)} %all-gather.4.cloned.1.call-done), calls=%async_computation.2 | async-start | bytes 4718592 | tf_op jit(solution)/shard_map/all_to_all | solution.py:93
  265.6 1.1 copy-start.2
  265.6 1.2 copy-start.5
  265.6 1.2 copy-start.7
  266.9 0.9 copy-start.8
  266.9 1.0 copy-start.9
Sparse Core Ops, SparseCore 0:
  170.0 48.6 all-gather.3
  220.2 22.3 all-gather.5
where the time goes:
time: 277 us; the launch traced here: 276 us
  blocking collectives  100 us (36%)
  waiting for transfers between devices  79.1 us (29%)
  local copies, waits for them, and re-layouts  50.8 us (18%)
  starting transfers between devices  13.7 us (5%)
  between operations  13.7 us (5%)
  matrix products  13.2 us (5%)
  other arithmetic  5.45 us (2%)
    all_gather x1, waiting for transfers between devices, shards(): right_cols = lax.all_gather(right_tri, 'row', axis=0, tiled=True)  48 us
    all_gather x1, blocking collectives, shards(): lax.all_gather(right_side, 'row', axis=0, tiled=True)  45.3 us
    all_gather x1, blocking collectives, shards(): lax.all_gather(mask_wire, 'row', axis=0, tiled=True)  35.2 us
    all_gather x1, waiting for transfers between devices, shards(): lax.all_gather(left_tri, 'col', axis=1, tiled=True)  18.8 us
    convert_element_type x1, local copies, waits for them, and re-layouts, shards(): outer = outer.reshape(block_rows, narrow, block_cols, narrow).transpose(0...  17.8 us
    all_gather x1, blocking collectives, shards(): lax.all_gather(left_side, 'col', axis=1, tiled=True)  13.4 us
    reshape x1, local copies, waits for them, and re-layouts, shards(): outer = outer.reshape(block_rows, block_cols, narrow * narrow)  12.7 us
    all_to_all x1, waiting for transfers between devices, shards(): lax.all_to_all(right_cols, 'col', split_axis=0, concat_axis=1, tiled=True)  11.6 us
  transfers between devices with their start and end apart: 5, of which 3 were waited for; matrix products, arithmetic and copies ran while one was open for 5% of the time, Pallas kernels for 0%

commit v1 on v0

--- a/solution.py
+++ b/solution.py
@@ -4,6 +4,20 @@
 from jax.sharding import PartitionSpec as P
 
 epsilon = 1e-05
+
+
+def _fill_panels(vals, inputs):
+    tmp = lax.axis_size("col")
+    row_out, outcome_arr = (tmp, lax.axis_index("col"))
+    so_far_all = [(no, (no - 1) % row_out) for no in range(row_out)]
+    before = vals.shape[1]
+    prior = vals
+    inter = inputs(prior, outcome_arr * before)
+    for rr in [*range(1, row_out)]:
+        prior = lax.ppermute(prior, "col", so_far_all)
+        current_block = inputs(prior, (outcome_arr + rr) % row_out * before)
+        inter = inter + current_block
+    return inter
 
 
 def normalize(values):
@@ -91,11 +105,14 @@
     ).astype(jnp.bfloat16)
     right_cols = lax.all_gather(right_tri, "row", axis=0, tiled=True)
     right_rows = lax.all_to_all(right_cols, "col", split_axis=0, concat_axis=1, tiled=True)
-    summed = jnp.einsum(
-        "ikc,jkc->ijc",
-        lax.all_gather(left_tri, "col", axis=1, tiled=True),
-        right_rows,
-        preferred_element_type=jnp.float32,
+    summed = _fill_panels(
+        left_tri,
+        lambda part, at: jnp.einsum(
+            "ikc,jkc->ijc",
+            part,
+            lax.dynamic_slice_in_dim(right_rows, at, part.shape[1], axis=1),
+            preferred_element_type=jnp.float32,
+        ),
     )
     normed_sum = normalize(summed).astype(jnp.bfloat16)
     update = jax.nn.sigmoid(

time: 277 us -> 296 us (1.069)
  local copies, waits for them, and re-layouts: 50.8 us -> 58.5 us
  starting transfers between devices: 13.7 us -> 19.1 us
  matrix products: 13.2 us -> 17.2 us
    ppermute x0 -> x3, waiting for transfers between devices: none -> 32 us  [_fill_panels(): prior = lax.ppermute(prior, 'col', so_far_all)]
    all_gather x1 -> x0, waiting for transfers between devices: 18.8 us -> none  [shards(): lax.all_gather(left_tri, 'col', axis=1, tiled=True)]
    all_to_all x1, waiting for transfers between devices: 11.6 us -> 0.01 us  [shards(): lax.all_to_all(right_cols, 'col', split_axis=0, concat_axis=1, tiled=True)]
    unnamed x33 -> x47, local copies, waits for them, and re-layouts: 6.54 us -> 13.9 us
    ppermute x0 -> x3, local copies, waits for them, and re-layouts: none -> 5.66 us  [_fill_panels(): prior = lax.ppermute(prior, 'col', so_far_all)]
    ppermute x0 -> x3, starting transfers between devices: none -> 5.63 us  [_fill_panels(): prior = lax.ppermute(prior, 'col', so_far_all)]
    all_to_all x2 -> x1, local copies, waits for them, and re-layouts: 5.89 us -> 0.71 us  [shards(): lax.all_to_all(right_cols, 'col', split_axis=0, concat_axis=1, tiled=True)]
    dot_general x1 -> x4, matrix products: 2.35 us -> 5.48 us  [shards(): jnp.einsum('ikc,jkc->ijc', part, lax.dynamic_slice_in_dim(right_rows, at,...]
  transfers between devices with their start and end apart: 5 -> 7, of which waited for: 3 -> 3; matrix products, arithmetic and copies ran while one was open for 5% -> 7% of each run, Pallas kernels for 0% -> 0%
where the time goes in v1:
time: 296 us; the launch traced here: 295 us
  blocking collectives  100 us (34%)
  waiting for transfers between devices  80.8 us (27%)
  local copies, waits for them, and re-layouts  58.5 us (20%)
  starting transfers between devices  19.1 us (6%)
  matrix products  17.2 us (6%)
  between operations  13.8 us (5%)
  other arithmetic  5.36 us (2%)
    all_gather x1, waiting for transfers between devices, shards(): right_cols = lax.all_gather(right_tri, 'row', axis=0, tiled=True)  48.8 us
    all_gather x1, blocking collectives, shards(): lax.all_gather(right_side, 'row', axis=0, tiled=True)  45.3 us
    all_gather x1, blocking collectives, shards(): lax.all_gather(mask_wire, 'row', axis=0, tiled=True)  35.2 us
    ppermute x3, waiting for transfers between devices, _fill_panels(): prior = lax.ppermute(prior, 'col', so_far_all)  32 us
    convert_element_type x1, local copies, waits for them, and re-layouts, shards(): outer = outer.reshape(block_rows, narrow, block_cols, narrow).transpose(0...  17.8 us
    unnamed x47, local copies, waits for them, and re-layouts  13.9 us
    all_gather x1, blocking collectives, shards(): lax.all_gather(left_side, 'col', axis=1, tiled=True)  13.4 us
    reshape x1, local copies, waits for them, and re-layouts, shards(): outer = outer.reshape(block_rows, block_cols, narrow * narrow)  12.7 us
  transfers between devices with their start and end apart: 7, of which 3 were waited for; matrix products, arithmetic and copies ran while one was open for 7% of the time, Pallas kernels for 0%

profile of v1, /device:TPU:0, one launch (start us, length us, event | category | flops | bytes accessed | tf_op | source)
XLA Modules:
  0.0 294.9 jit_solution(18066530004756536214)
XLA Ops:
  7.4 6.2 %all-gather = bf16[4,48,32]{1,2,0:T(8,128)(2,1)S(1)} all-gather(bf16[1,48,32]{1,2,0:T(8,128)(2,1)S(1)} %bitcast.99), channel_id=1, replica_groups=mesh['row'=8,'col'=4] {'col'}, dimensions={0}, use_global_device_ids=true | all-gather | bytes 15360 | tf_op jit(solution)/shard_map/all_gather | solution.py:64
  14.5 6.2 %all-to-all-start.1 = ((bf16[8,2,384]{2,1,0:T(2,128)(2,1)}), bf16[8,2,384]{2,1,0:T(2,128)(2,1)S(1)}, u32[]{:S(2)}, u32[]{:S(2)}) async-start(bf16[8,2,384]{2,1,0:T(2,128)(2,1)} %reshape.110), calls=%async_computation.1 | async-start | bytes 24576 | tf_op jit(solution)/shard_map/all_to_all | solution.py:68
  20.8 1.4 convert_reduce_fusion
  24.1 13.4 %all_gather.15 = bf16[32,192,32]{2,0,1:T(8,128)(2,1)} all-gather(bf16[32,48,32]{2,0,1:T(8,128)(2,1)S(1)} %copy.72), channel_id=1, replica_groups=mesh['row'=8,'col'=4] {'col'}, dimensions={1}, use_global_device_ids=true | all-gather | bytes 491520 | tf_op jit(solution)/shard_map/all_gather | solution.py:63
  38.1 45.3 %all_gather.16 = bf16[256,48,32]{1,2,0:T(8,128)(2,1)S(1)} all-gather(bf16[32,48,32]{1,2,0:T(8,128)(2,1)S(1)} %fusion.17), channel_id=1, replica_groups=mesh['row'=8,'col'=4] {'row'}, dimensions={0}, use_global_device_ids=true | all-gather | bytes 884736 | tf_op jit(solution)/shard_map/all_gather | solution.py:59
  83.6 3.8 %reshape.108 = bf16[8,2,12288]{2,1,0:T(2,128)(2,1)} reshape(bf16[192,32,32]{2,1,0:T(8,128)(2,1)} %bitcast.95) | data formatting | bytes 786432
  87.4 2.4 copy.77
  89.8 3.6 %all-to-all-start = ((bf16[8,2,12288]{2,1,0:T(2,128)(2,1)}), bf16[8,2,12288]{2,1,0:T(2,128)(2,1)S(1)}, u32[]{:S(2)}, u32[]{:S(2)}) async-start(bf16[8,2,12288]{2,1,0:T(2,128)(2,1)} %reshape.108), calls=%async_computation | async-start | bytes 786432 | tf_op jit(solution)/shard_map/all_to_all | solution.py:67
  93.4 35.2 %all_gather.18 = bf16[256,48]{1,0:T(8,128)(2,1)S(1)} all-gather(bf16[32,48]{1,0:T(8,128)(2,1)S(1)} %get-tuple-element.11), channel_id=1, replica_groups=mesh['row'=8,'col'=4] {'row'}, dimensions={0}, use_global_device_ids=true | all-gather | bytes 27648 | tf_op jit(solution)/shard_map/all_gather | solution.py:60
  131.6 3.7 %convert_bitcast_fusion = bf16[24,48,32,32]{1,2,3,0:T(8,128)(2,1)} fusion(bf16[24,32,256,1]{2,1,3,0:T(8,128)(2,1)S(1)} %bitcast.96, bf16[48,32,256]{2,0,1:T(8,128)(2,1)S(1)} %copy-done.5), kind=kOutput, calls=%fused_computation | convolution fusion | flops 605159424 | bytes 3538944 | tf_op jit(solution)/shard_map/dot_general | solution.py:72
  135.4 17.8 %copy.78 = bf16[24,48,32,32]{3,2,1,0:T(8,128)(2,1)} copy(bf16[24,48,32,32]{1,2,3,0:T(8,128)(2,1)} %convert_bitcast_fusion) | data formatting | bytes 4718592 | tf_op jit(solution)/shard_map/convert_element_type | solution.py:81
  153.2 12.7 %reshape.95 = bf16[24,48,1024]{2,1,0:T(8,128)(2,1)S(1)} reshape(bf16[24,48,32,32]{3,2,1,0:T(8,128)(2,1)} %copy.78) | data formatting | bytes 4718592 | tf_op jit(solution)/shard_map/reshape | solution.py:83
  165.9 1.8 fusion.49
  168.8 1.1 fusion.22
  169.9 48.8 %all-gather.3.cloned.1.call-done = bf16[192,48,128]{2,1,0:T(8,128)(2,1)} async-done(((bf16[24,48,128]{2,1,0:T(8,128)(2,1)}), bf16[192,48,128]{2,1,0:T(8,128)(2,1)}) %all-gather.3.cloned.1.call-update) | async-done | bytes 2359312 | tf_op jit(solution)/shard_map/all_gather | solution.py:106
  218.6 3.6 %all-to-all-start.2 = ((bf16[192,48,128]{2,1,0:T(8,128)(2,1)}), bf16[192,48,128]{2,1,0:T(8,128)(2,1)S(1)}, u32[]{:S(2)}, u32[]{:S(2)}) async-start(bf16[192,48,128]{2,1,0:T(8,128)(2,1)} %all-gather.3.cloned.1.call-done), calls=%async_computation.2 | async-start | bytes 4718592 | tf_op jit(solution)/shard_map/all_to_all | solution.py:107
  222.3 1.7 collective-permute-start
  224.0 27.8 %collective-permute-done = bf16[24,48,128]{2,1,0:T(8,128)(2,1)S(1)} collective-permute-done((bf16[24,48,128]{2,1,0:T(8,128)(2,1)S(1)}, bf16[24,48,128]{2,1,0:T(8,128)(2,1)S(1)}, u32[]{:S(2)}, u32[]{:S(2)}) %collective-permute-start) | collective-permute-done | bytes 294944 | tf_op jit(solution)/shard_map/ppermute | solution.py:17
  252.5 1.9 collective-permute-start.1
  254.4 4.2 %collective-permute-done.1 = bf16[24,48,128]{2,1,0:T(8,128)(2,1)} collective-permute-done((bf16[24,48,128]{2,1,0:T(8,128)(2,1)S(1)}, bf16[24,48,128]{2,1,0:T(8,128)(2,1)}, u32[]{:S(2)}, u32[]{:S(2)}) %collective-permute-start.1) | collective-permute-done | bytes 294944 | tf_op jit(solution)/shard_map/ppermute | solution.py:17
  258.7 2.0 collective-permute-start.2
  260.7 1.3 copy.84
  262.0 2.1 fusion.9
  264.1 1.2 copy.86
  265.3 2.2 copy.88
  267.5 2.2 copy.90
  270.5 1.4 constant_dynamic-slice_fusion
  271.8 1.7 copy.98
  273.5 1.7 copy.97
  276.2 1.8 copy.100
  278.0 2.7 fusion.52
  286.5 1.5 fusion.15
  (84 shorter events, 16.4 us)
Async XLA Ops:
  6.5 159.4 %copy-start = (bf16[1024,128]{1,0:T(8,128)(2,1)S(1)}, bf16[1024,128]{1,0:T(8,128)(2,1)}, u32[]{:S(2)}) copy-start(bf16[1024,128]{1,0:T(8,128)(2,1)} %param.18) | copy-start | bytes 786436
  6.5 15.7 %copy-start.4 = (bf16[32,48,256]{2,1,0:T(8,128)(2,1)S(1)}, bf16[32,48,256]{2,1,0:T(8,128)(2,1)}, u32[]{:S(2)}) copy-start(bf16[32,48,256]{2,1,0:T(8,128)(2,1)} %param.12) | copy-start | bytes 2359300
  6.5 16.2 %copy-start.16 = (bf16[256,32]{0,1:T(8,128)(2,1)S(1)}, bf16[256,32]{0,1:T(8,128)(2,1)}, u32[]{:S(2)}) copy-start(bf16[256,32]{0,1:T(8,128)(2,1)} %param.16) | copy-start | bytes 49156
  14.5 75.3 %all-to-all-start.1 = ((bf16[8,2,384]{2,1,0:T(2,128)(2,1)}), bf16[8,2,384]{2,1,0:T(2,128)(2,1)S(1)}, u32[]{:S(2)}, u32[]{:S(2)}) async-start(bf16[8,2,384]{2,1,0:T(2,128)(2,1)} %reshape.110), calls=%async_computation.1 | async-start | bytes 24576 | tf_op jit(solution)/shard_map/all_to_all | solution.py:68
  23.4 14.0 %copy-start.17 = (bf16[256,32]{0,1:T(8,128)(2,1)S(1)}, bf16[256,32]{0,1:T(8,128)(2,1)}, u32[]{:S(2)}) copy-start(bf16[256,32]{0,1:T(8,128)(2,1)} %param.17) | copy-start | bytes 49156
  38.1 45.4 %copy-start.18 = (s32[192]{0:T(256)S(1)}, s32[192]{0:T(256)}, u32[]{:S(2)}) copy-start(s32[192]{0:T(256)} %param.14) | copy-start | bytes 2308
  89.8 39.2 %all-to-all-start = ((bf16[8,2,12288]{2,1,0:T(2,128)(2,1)}), bf16[8,2,12288]{2,1,0:T(2,128)(2,1)S(1)}, u32[]{:S(2)}, u32[]{:S(2)}) async-start(bf16[8,2,12288]{2,1,0:T(2,128)(2,1)} %reshape.108), calls=%async_computation | async-start | bytes 786432 | tf_op jit(solution)/shard_map/all_to_all | solution.py:67
  93.4 125.3 %all-gather.3.cloned.1.call-start = ((), (), s32[]{:S(2)}) async-start(), calls=%async_computation.3 | async-start | bytes 2654208 | tf_op jit(solution)/shard_map/all_gather | solution.py:106
  130.4 1.2 copy-start.5
  165.9 2.3 copy-start.12
  167.8 94.2 %copy-start.2 = (f32[24,48,128]{2,1,0:T(8,128)}, f32[24,48,128]{2,1,0:T(8,128)S(1)}, u32[]{:S(2)}) copy-start(f32[24,48,128]{2,1,0:T(8,128)S(1)} %get-tuple-element.14) | copy-start | bytes 1769476
  218.6 51.1 %all-to-all-start.2 = ((bf16[192,48,128]{2,1,0:T(8,128)(2,1)}), bf16[192,48,128]{2,1,0:T(8,128)(2,1)S(1)}, u32[]{:S(2)}, u32[]{:S(2)}) async-start(bf16[192,48,128]{2,1,0:T(8,128)(2,1)} %all-gather.3.cloned.1.call-done), calls=%async_computation.2 | async-start | bytes 4718592 | tf_op jit(solution)/shard_map/all_to_all | solution.py:107
  222.3 29.5 %collective-permute-start = (bf16[24,48,128]{2,1,0:T(8,128)(2,1)S(1)}, bf16[24,48,128]{2,1,0:T(8,128)(2,1)S(1)}, u32[]{:S(2)}, u32[]{:S(2)}) collective-permute-start(bf16[24,48,128]{2,1,0:T(8,128)(2,1)S(1)} %get-tuple-element.5), channel_id=1, source_target_pairs={{0,3},{1,0},{2,1},{3,2},{4,7},{5,4},{6,5},{7,6},{8,11},{9,8},{10,9... | collective-permute-start | bytes 884744 | tf_op jit(solution)/shard_map/ppermute | solution.py:17
  251.8 0.7 copy-start.10
  252.5 6.1 %collective-permute-start.1 = (bf16[24,48,128]{2,1,0:T(8,128)(2,1)S(1)}, bf16[24,48,128]{2,1,0:T(8,128)(2,1)}, u32[]{:S(2)}, u32[]{:S(2)}) collective-permute-start(bf16[24,48,128]{2,1,0:T(8,128)(2,1)S(1)} %collective-permute-done), channel_id=1, source_target_pairs={{0,3},{1,0},{2,1},{3,2},{4,7},{5,4},{6,5},{7,6},{8,11},{9,8},{10,9... | collective-permute-start | bytes 884744 | tf_op jit(solution)/shard_map/ppermute | solution.py:17
  258.7 8.9 %collective-permute-start.2 = (bf16[24,48,128]{2,1,0:T(8,128)(2,1)}, bf16[24,48,128]{2,1,0:T(8,128)(2,1)}, u32[]{:S(2)}, u32[]{:S(2)}) collective-permute-start(bf16[24,48,128]{2,1,0:T(8,128)(2,1)} %collective-permute-done.1), channel_id=1, source_target_pairs={{0,3},{1,0},{2,1},{3,2},{4,7},{5,4},{6,5},{7,6},{8,11},{9,8},{10,9... | collective-permute-start | bytes 884744 | tf_op jit(solution)/shard_map/ppermute | solution.py:17
  261.9 2.1 copy-start.11
  278.0 2.7 copy-start.1
  278.0 2.7 copy-start.7
  280.7 1.1 copy-start.8
  281.9 1.1 copy-start.6
  284.3 1.1 copy-start.3
  284.3 1.2 copy-start.9
  284.3 1.2 copy-start.13
  285.5 0.9 copy-start.14
  285.5 1.0 copy-start.15
Sparse Core Ops, SparseCore 0:
  170.0 48.6 all-gather.2
